TPU v7x, 32 devices: a whole 2x2x4 slice. The times are simulated.
32 devices in a mesh: dp: 4 (over z), vocab: 8 (over y, x, core).
Axes of the slice: x: 2, y: 2, z: 4, core: 2. Of those that a mesh axis runs over, the one named last changes fastest.
Arguments:
- base_hidden: bfloat16 [96, 8192], P('dp', 'vocab'), may hold values from -16 to 16
- reinforced_hidden: bfloat16 [96, 8192], P('dp', 'vocab'), may hold values from -16 to 16
- trained_hidden: bfloat16 [96, 8192], P('dp', 'vocab'), may hold values from -16 to 16
- frozen_head: bfloat16 [8192, 16384], P(None, ('dp', 'vocab')), may hold values from -1 to 1
- trained_head: bfloat16 [8192, 16384], P(None, ('dp', 'vocab')), may hold values from -1 to 1
- label_tokens: int32 [96], P('dp'), may hold values from 0 to 16383
- generic_map: int32 [16384], replicated, may hold values from 0 to 16383, as said below
- loss_mask: int32 [96], P('dp'), may hold values 0 or 1
Outputs:
- token_loss: float32 [96], P('dp')
- head_grad: bfloat16 [8192, 16384], P(None, ('dp', 'vocab'))
- hidden_grad: bfloat16 [96, 8192], P('dp', 'vocab')
Inputs may be any that keep to these rules, and one draw needn't show every extreme that they name: `generic_map`: maps each token to its generic counterpart; many tokens map to themselves.
All inputs are finite; a program needn't handle non-finite values. No bound on the sum of `loss_mask` on one device may be relied on, other than what follows from the above.
Results may differ from a plain program's by a relative error of at most 0.0065.
Values may be sent and summed in bfloat16 or wider, within the bound.
No kernel may reach another device: no remote copies, remote signals or barrier semaphores. Data moves between devices by JAX's collectives and lax.ppermute only.
A program may use at most 128 MiB of HBM per device.

v0:
```python
import jax
import jax.numpy as jnp
from jax import lax
from jax.sharding import PartitionSpec as P

reinforce_weight = 2.0
anchor_share = 0.3
loss_scale = 16.0


def on_device(
    base_hidden,
    reinforced_hidden,
    trained_hidden,
    frozen_head,
    trained_head,
    label_tokens,
    generic_map,
    loss_mask,
):
    tok_local = base_hidden.shape[0]
    feature_local = base_hidden.shape[1]
    dp_count = lax.axis_size("dp")
    vocab_count = lax.axis_size("vocab")
    wide_rows = (
        lax.all_gather(base_hidden, "vocab", axis=1, tiled=True),
        lax.all_gather(reinforced_hidden, "vocab", axis=1, tiled=True),
        lax.all_gather(trained_hidden, "vocab", axis=1, tiled=True),
    )
    base_rows, reinforced_rows, trained_rows = (
        lax.all_gather(wide_rows[0], "dp", axis=0, tiled=True),
        lax.all_gather(wide_rows[1], "dp", axis=0, tiled=True),
        lax.all_gather(wide_rows[2], "dp", axis=0, tiled=True),
    )
    all_labels = (
        lax.all_gather(label_tokens, "dp", axis=0, tiled=True),
        lax.all_gather(loss_mask, "dp", axis=0, tiled=True),
    )
    labels_all, mask_all = all_labels
    base_logits = jnp.dot(base_rows, frozen_head, preferred_element_type=jnp.float32)
    reinforced_logits = jnp.dot(reinforced_rows, frozen_head, preferred_element_type=jnp.float32)
    generic = base_logits - reinforce_weight * jnp.maximum(reinforced_logits - base_logits, 0.0)
    trained_logits = jnp.dot(trained_rows, trained_head, preferred_element_type=jnp.float32)
    vocab_local = trained_head.shape[1]
    vocab_start = lax.axis_index(("dp", "vocab")) * vocab_local
    anchor = generic_map[labels_all]
    anchor_hit = (vocab_start + lax.iota(jnp.int32, vocab_local))[None, :] == anchor[:, None]
    picked_local = jnp.sum(jnp.where(anchor_hit, trained_logits, 0.0), axis=1)
    generic_peak, trained_peak = lax.pmax(
        (jnp.max(generic, axis=1), jnp.max(trained_logits, axis=1)), ("dp", "vocab")
    )
    generic_exps = jnp.exp(generic - generic_peak[:, None])
    trained_exps = jnp.exp(trained_logits - trained_peak[:, None])
    generic_total, cross_term, trained_total, picked_logit = lax.psum(
        (
            jnp.sum(generic_exps, axis=1),
            jnp.sum(generic_exps * trained_logits, axis=1),
            jnp.sum(trained_exps, axis=1),
            picked_local,
        ),
        ("dp", "vocab"),
    )
    token_weight = mask_all.astype(jnp.float32)
    loss_all = token_weight * (
        trained_peak
        + jnp.log(trained_total)
        - (1.0 - anchor_share) * cross_term / generic_total
        - anchor_share * picked_logit
    )
    token_loss = lax.dynamic_slice_in_dim(loss_all, lax.axis_index("dp") * tok_local, tok_local, 0)
    target = (1.0 - anchor_share) * generic_exps / generic_total[
        :, None
    ] + anchor_share * anchor_hit.astype(jnp.float32)
    logit_grad = (
        loss_scale * token_weight[:, None] * (trained_exps / trained_total[:, None] - target)
    ).astype(jnp.bfloat16)
    head_total = lax.dot_general(
        trained_rows, logit_grad, (((0,), (0,)), ((), ())), preferred_element_type=jnp.float32
    )
    grad_blocks = logit_grad.reshape(dp_count, tok_local, vocab_local)
    head_blocks = trained_head.reshape(vocab_count, feature_local, vocab_local)
    hidden_terms = jnp.einsum(
        "atv,bdv->abtd", grad_blocks, head_blocks, preferred_element_type=jnp.float32
    )
    hidden_terms = hidden_terms.reshape(dp_count * vocab_count * tok_local, feature_local)
    hidden_total = lax.psum_scatter(hidden_terms, ("dp", "vocab"), scatter_dimension=0, tiled=True)
    return (token_loss, head_total.astype(jnp.bfloat16), hidden_total.astype(jnp.bfloat16))


def solution(mesh):
    placed = (
        P("dp", "vocab"),
        P("dp", "vocab"),
        P("dp", "vocab"),
        P(None, ("dp", "vocab")),
        P(None, ("dp", "vocab")),
        P("dp"),
        P(),
        P("dp"),
    )
    return jax.shard_map(
        on_device,
        mesh=mesh,
        in_specs=placed,
        out_specs=(P("dp"), P(None, ("dp", "vocab")), P("dp", "vocab")),
        check_vma=False,
    )
```

profile of v0, /device:TPU:0, one launch (start us, length us, event | category | flops | bytes accessed | tf_op | source)
XLA Modules:
  0.0 336.3 jit_solution(8015253757386036704)
XLA Ops:
  7.2 0.0 copy-start
  7.2 0.0 all-gather.6.cloned.1.call-start
  7.2 12.9 %all_gather.27 = bf16[24,8192]{1,0:T(8,128)(2,1)} all-gather(bf16[24,1024]{1,0:T(8,128)(2,1)} %param.8), channel_id=1, replica_groups=mesh['dp'=4,'vocab'=8] {'vocab'}, dimensions={1}, use_global_device_ids=true | all-gather | bytes 442368 | tf_op jit(solution)/shard_map/all_gather | solution.py:26
  20.1 0.0 all-gather.6.cloned.1.call-update
  20.2 0.0 all-gather.8.cloned.1.call-start
  20.2 10.5 %all_gather.29 = bf16[24,8192]{1,0:T(8,128)(2,1)} all-gather(bf16[24,1024]{1,0:T(8,128)(2,1)} %param.9), channel_id=1, replica_groups=mesh['dp'=4,'vocab'=8] {'vocab'}, dimensions={1}, use_global_device_ids=true | all-gather | bytes 442368 | tf_op jit(solution)/shard_map/all_gather | solution.py:27
  30.7 0.0 all-gather.8.cloned.1.call-update
  30.7 0.0 all-gather.4.cloned.1.call-start
  30.7 10.5 %all_gather.25 = bf16[24,8192]{1,0:T(8,128)(2,1)} all-gather(bf16[24,1024]{1,0:T(8,128)(2,1)} %param.10), channel_id=1, replica_groups=mesh['dp'=4,'vocab'=8] {'vocab'}, dimensions={1}, use_global_device_ids=true | all-gather | bytes 442368 | tf_op jit(solution)/shard_map/all_gather | solution.py:28
  41.2 0.0 all-gather.4.cloned.1.call-update
  41.2 0.0 reduce-scatter.2.cloned.1.call-start
  41.3 1.2 dynamic-slice
  43.2 0.9 dynamic-update-slice.1
  44.1 0.8 dynamic-update-slice
  44.9 9.1 %all-reduce.2 = (s32[96]{0:T(128)S(1)}, s32[96]{0:T(128)S(1)}) all-reduce(s32[96]{0:T(128)S(1)} %dynamic-update-slice.1, s32[96]{0:T(128)S(1)} %dynamic-update-slice), channel_id=1, replica_groups=mesh['dp'=4,'vocab'=8] {'dp'}, use_global_device_ids=true, to_apply=%add.1 | all-reduce | flops 192 | bytes 1536
  54.1 0.0 copy-done
  54.1 1.1 gather_fusion
  55.2 2.5 all-gather.6.cloned.1.call-done
  57.8 5.3 %fusion.13 = f32[96,512]{1,0:T(8,128)S(1)} fusion(bf16[96,8192]{1,0:T(8,128)(2,1)} %all-gather.6.cloned.1.call-done, bf16[8192,512]{1,0:T(8,128)(2,1)} %param.11), kind=kOutput, calls=%fused_computation.26 | convolution fusion | flops 805306368 | bytes 10158080 | tf_op jit(solution)/shard_map/dot_general | solution.py:40
  63.1 32.2 %all-gather.8.cloned.1.call-done = bf16[96,8192]{1,0:T(8,128)(2,1)} async-done(((bf16[24,8192]{1,0:T(8,128)(2,1)}), bf16[96,8192]{1,0:T(8,128)(2,1)}) %all-gather.8.cloned.1.call-update) | async-done | bytes 1572880 | tf_op jit(solution)/shard_map/all_gather | solution.py:32
  95.3 5.4 %fusion.12 = (f32[96]{0:T(128)S(1)}, f32[96,512]{1,0:T(8,128)S(1)}) fusion(f32[96,512]{1,0:T(8,128)S(1)} %fusion.13, bf16[96,8192]{1,0:T(8,128)(2,1)} %all-gather.8.cloned.1.call-done, bf16[8192,512]{1,0:T(8,128)(2,1)} %param.11), kind=kOutput, calls=%fused_computation.25 | convolution fusion | flops 805552000 | bytes 10355072 | tf_op jit(solution)/shard_map/dot_general | solution.py:41
  100.7 32.1 %all-gather.4.cloned.1.call-done = bf16[96,8192]{1,0:T(8,128)(2,1)} async-done(((bf16[24,8192]{1,0:T(8,128)(2,1)}), bf16[96,8192]{1,0:T(8,128)(2,1)}) %all-gather.4.cloned.1.call-update) | async-done | bytes 1572880 | tf_op jit(solution)/shard_map/all_gather | solution.py:33
  132.8 5.4 %fusion.11 = (f32[96]{0:T(128)S(1)}, f32[96,512]{1,0:T(8,128)S(1)}) fusion(bf16[96,8192]{1,0:T(8,128)(2,1)} %all-gather.4.cloned.1.call-done, bf16[8192,512]{1,0:T(8,128)(2,1)} %param.12), kind=kOutput, calls=%fused_computation.24 | convolution fusion | flops 805355392 | bytes 10158464 | tf_op jit(solution)/shard_map/dot_general | solution.py:43
  138.2 39.2 %all-reduce.4 = (f32[96]{0:T(128)S(1)}, f32[96]{0:T(128)S(1)}) all-reduce(f32[96]{0:T(128)S(1)} %get-tuple-element.25, f32[96]{0:T(128)S(1)} %get-tuple-element.27), channel_id=1, replica_groups=mesh['dp'=4,'vocab'=8] {'dp','vocab'}, use_global_device_ids=true, to_apply=%region_1.2 | all-reduce | flops 192 | bytes 1536 | tf_op jit(solution)/shard_map/pmax | solution.py:49
  177.4 0.3 fusion.9
  177.7 40.1 %all-reduce.3 = (f32[96]{0:T(128)S(1)}, f32[96]{0:T(128)S(1)}, f32[96]{0:T(128)S(1)}, f32[96]{0:T(128)S(1)}) all-reduce(f32[96]{0:T(128)S(1)} %get-tuple-element.12, f32[96]{0:T(128)S(1)} %get-tuple-element.13, f32[96]{0:T(128)S(1)} %get-tuple-element.14, f32[96]{0:T(128)S(1)} %get-tuple-element.11), channel_id=1, replica_groups=mesh['dp'=4,'vocab'=8] {'dp','vocab'}, use_global_device_ids=true, to_apply=%region_11.12 | all-reduce | flops 384 | bytes 3072 | tf_op jit(solution)/shard_map/psum | solution.py:54
  217.8 0.2 fusion.8
  218.0 0.0 copy-start.1
  218.0 7.9 %fusion.14 = f32[4,24,8,1024]{3,1,2,0:T(8,128)} fusion(bf16[4,24,512,1]{2,1,3,0:T(8,128)(2,1)S(1)} %bitcast.26, bf16[8,1024,512,1]{2,1,0,3:T(8,128)(2,1)} %bitcast.24), kind=kOutput, calls=%fused_computation.27 | convolution fusion | flops 805306368 | bytes 11632640 | tf_op jit(solution)/shard_map/atv,bdv->abtd/dot_general | solution.py:82
  225.9 0.0 reduce-scatter.2.cloned.1.call-update
  225.9 0.0 copy-done.1
  226.0 5.6 %fusion = bf16[8192,512]{0,1:T(8,128)(2,1)} fusion(bf16[96,512]{1,0:T(8,128)(2,1)S(1)} %fusion.8, bf16[96,8192]{1,0:T(8,128)(2,1)S(1)} %copy-done.1), kind=kOutput, calls=%fused_computation.2 | convolution fusion | flops 809500672 | bytes 10059776 | tf_op jit(solution)/shard_map/dot_general | solution.py:77
  231.5 12.0 %copy.12 = bf16[8192,512]{1,0:T(8,128)(2,1)} copy(bf16[8192,512]{0,1:T(8,128)(2,1)} %fusion) | data formatting | bytes 16777216
  243.6 0.6 dynamic_slice.3
  244.2 84.1 %reduce-scatter.2.cloned.1.call-done = f32[24,1024]{1,0:T(8,128)} async-done(((f32[768,1024]{1,0:T(8,128)}), f32[24,1024]{1,0:T(8,128)}) %reduce-scatter.2.cloned.1.call-update) | async-done | bytes 98320 | tf_op jit(solution)/shard_map/reduce_scatter | solution.py:86
  328.2 1.5 convert_element_type.20
  (6 shorter events, 0.0 us)
Async XLA Ops:
  7.2 46.9 %copy-start = (s32[16384]{0:T(1024)S(1)}, s32[16384]{0:T(1024)}, u32[]{:S(2)}) copy-start(s32[16384]{0:T(1024)} %param.14) | copy-start | bytes 196612
  7.2 50.6 %all-gather.6.cloned.1.call-start = ((), (), s32[]{:S(2)}) async-start(), calls=%async_computation.2 | async-start | bytes 1966080 | tf_op jit(solution)/shard_map/all_gather | solution.py:31
  20.2 75.1 %all-gather.8.cloned.1.call-start = ((), (), s32[]{:S(2)}) async-start(), calls=%async_computation.3 | async-start | bytes 1966080 | tf_op jit(solution)/shard_map/all_gather | solution.py:32
  30.7 102.1 %all-gather.4.cloned.1.call-start = ((), (), s32[]{:S(2)}) async-start(), calls=%async_computation.1 | async-start | bytes 1966080 | tf_op jit(solution)/shard_map/all_gather | solution.py:33
  41.2 287.0 %reduce-scatter.2.cloned.1.call-start = ((), (), s32[]{:S(2)}) async-start(), calls=%async_computation.4 | async-start | bytes 3244032 | tf_op jit(solution)/shard_map/reduce_scatter | solution.py:86
  218.0 8.0 %copy-start.1 = (bf16[96,8192]{1,0:T(8,128)(2,1)S(1)}, bf16[96,8192]{1,0:T(8,128)(2,1)}, u32[]{:S(2)}) copy-start(bf16[96,8192]{1,0:T(8,128)(2,1)} %all-gather.4.cloned.1.call-done) | copy-start | bytes 4718596
Sparse Core Ops, SparseCore 0:
  20.3 37.4 all-gather.5
  59.3 35.8 all-gather.7
  96.8 35.8 all-gather.3
  226.1 102.1 reduce-scatter.1
where the time goes:
time: 337 us; the launch traced here: 336 us
  waiting for transfers between devices  151 us (45%)
  blocking collectives  122 us (36%)
  matrix products  29.7 us (9%)
  local copies, waits for them, and re-layouts  16.7 us (5%)
  between operations  14.5 us (4%)
    reduce_scatter x1, waiting for transfers between devices, on_device(): lax.psum_scatter(hidden_terms, ('dp', 'vocab'), scatter_dimension=0, tile...  84.1 us
    psum x1, blocking collectives, on_device(): lax.psum((jnp.sum(generic_exps, axis=1), jnp.sum(generic_exps * trained_l...  40.1 us
    pmax x1, blocking collectives, on_device(): lax.pmax((jnp.max(generic, axis=1), jnp.max(trained_logits, axis=1)), ('d...  39.2 us
    all_gather x1, waiting for transfers between devices, on_device(): lax.all_gather(wide_rows[1], 'dp', axis=0, tiled=True)  32.2 us
    all_gather x1, waiting for transfers between devices, on_device(): lax.all_gather(wide_rows[2], 'dp', axis=0, tiled=True)  32.1 us
    unnamed x10, local copies, waits for them, and re-layouts  15 us
    all_gather x1, blocking collectives, on_device(): lax.all_gather(base_hidden, 'vocab', axis=1, tiled=True)  12.9 us
    all_gather x1, blocking collectives, on_device(): lax.all_gather(trained_hidden, 'vocab', axis=1, tiled=True)  10.5 us
  transfers between devices with their start and end apart: 4, of which 4 were waited for; matrix products, arithmetic and copies ran while one was open for 10% of the time, Pallas kernels for 0%

commit v1 on v0

--- a/solution.py
+++ b/solution.py
@@ -6,6 +6,19 @@
 reinforce_weight = 2.0
 anchor_share = 0.3
 loss_scale = 16.0
+
+
+def ring_gather(array, axis, dim):
+    count, mine, rows = (lax.axis_size(axis), lax.axis_index(axis), array.shape[dim])
+    upward = [(i, (i + 1) % count) for i in range(count)]
+    whole = jnp.zeros((*array.shape[:dim], count * rows, *array.shape[dim + 1 :]), array.dtype)
+    held = array
+    for step in range(count):
+        source = (mine - step) % count
+        whole = lax.dynamic_update_slice_in_dim(whole, held, source * rows, axis=dim)
+        if step < count - 1:
+            held = lax.ppermute(held, axis, upward)
+    return whole
 
 
 def on_device(
@@ -29,7 +42,7 @@
     )
     base_rows, reinforced_rows, trained_rows = (
         lax.all_gather(wide_rows[0], "dp", axis=0, tiled=True),
-        lax.all_gather(wide_rows[1], "dp", axis=0, tiled=True),
+        ring_gather(wide_rows[1], "dp", 0),
         lax.all_gather(wide_rows[2], "dp", axis=0, tiled=True),
     )
     all_labels = (

time: 337 us -> 318 us (0.944)
  waiting for transfers between devices: 151 us -> 120 us
  starting transfers between devices: 0.16 us -> 12.4 us
    all_gather x1 -> x0, waiting for transfers between devices: 32.2 us -> none  [on_device(): lax.all_gather(wide_rows[1], 'dp', axis=0, tiled=True)]
    ppermute x0 -> x3, waiting for transfers between devices: none -> 29.4 us  [ring_gather(): held = lax.ppermute(held, axis, upward)]
    all_gather x1, waiting for transfers between devices: 32.1 us -> 7.64 us  [on_device(): lax.all_gather(wide_rows[2], 'dp', axis=0, tiled=True)]
    ppermute x0 -> x3, starting transfers between devices: none -> 12.3 us  [ring_gather(): held = lax.ppermute(held, axis, upward)]
    unnamed x10 -> x16, local copies, waits for them, and re-layouts: 15 us -> 14.5 us
  transfers between devices with their start and end apart: 4 -> 6, of which waited for: 4 -> 4; matrix products, arithmetic and copies ran while one was open for 10% -> 10% of each run, Pallas kernels for 0% -> 0%
where the time goes in v1:
time: 318 us; the launch traced here: 317 us
  blocking collectives  122 us (38%)
  waiting for transfers between devices  120 us (38%)
  matrix products  29.1 us (9%)
  local copies, waits for them, and re-layouts  16.5 us (5%)
  between operations  14.7 us (5%)
  starting transfers between devices  12.4 us (4%)
    reduce_scatter x1, waiting for transfers between devices, on_device(): lax.psum_scatter(hidden_terms, ('dp', 'vocab'), scatter_dimension=0, tile...  82.8 us
    psum x1, blocking collectives, on_device(): lax.psum((jnp.sum(generic_exps, axis=1), jnp.sum(generic_exps * trained_l...  40.8 us
    pmax x1, blocking collectives, on_device(): lax.pmax((jnp.max(generic, axis=1), jnp.max(trained_logits, axis=1)), ('d...  38.5 us
    ppermute x3, waiting for transfers between devices, ring_gather(): held = lax.ppermute(held, axis, upward)  29.4 us
    unnamed x16, local copies, waits for them, and re-layouts  14.5 us
    all_gather x1, blocking collectives, on_device(): lax.all_gather(base_hidden, 'vocab', axis=1, tiled=True)  12.9 us
    ppermute x3, starting transfers between devices, ring_gather(): held = lax.ppermute(held, axis, upward)  12.3 us
    unnamed x1, blocking collectives  10.7 us
  transfers between devices with their start and end apart: 6, of which 4 were waited for; matrix products, arithmetic and copies ran while one was open for 10% of the time, Pallas kernels for 0%

profile of v1, /device:TPU:0, one launch (start us, length us, event | category | flops | bytes accessed | tf_op | source)
XLA Modules:
  0.0 316.8 jit_solution(1416778297748360266)
XLA Ops:
  7.2 0.0 copy-start
  7.2 0.0 copy-start.4
  7.2 0.0 copy-start.2
  7.2 0.0 copy-start.3
  7.2 0.0 all-gather.5.cloned.1.call-start
  7.3 12.9 %all_gather.24 = bf16[24,8192]{1,0:T(8,128)(2,1)} all-gather(bf16[24,1024]{1,0:T(8,128)(2,1)} %param.8), channel_id=1, replica_groups=mesh['dp'=4,'vocab'=8] {'vocab'}, dimensions={1}, use_global_device_ids=true | all-gather | bytes 442368 | tf_op jit(solution)/shard_map/all_gather | solution.py:39
  20.2 0.0 all-gather.5.cloned.1.call-update
  20.2 0.0 all-gather.3.cloned.1.call-start
  20.2 8.9 %all_gather.26 = bf16[24,8192]{1,0:T(8,128)(2,1)S(1)} all-gather(bf16[24,1024]{1,0:T(8,128)(2,1)} %param.9), channel_id=1, replica_groups=mesh['dp'=4,'vocab'=8] {'vocab'}, dimensions={1}, use_global_device_ids=true | all-gather | bytes 442368 | tf_op jit(solution)/shard_map/all_gather | solution.py:40
  29.1 1.6 collective-permute-start
  30.7 10.4 %all_gather.22 = bf16[24,8192]{1,0:T(8,128)(2,1)} all-gather(bf16[24,1024]{1,0:T(8,128)(2,1)} %param.10), channel_id=1, replica_groups=mesh['dp'=4,'vocab'=8] {'vocab'}, dimensions={1}, use_global_device_ids=true | all-gather | bytes 442368 | tf_op jit(solution)/shard_map/all_gather | solution.py:41
  41.1 0.0 all-gather.3.cloned.1.call-update
  41.1 0.0 reduce-scatter.2.cloned.1.call-start
  41.3 0.0 copy-done.4
  41.3 0.6 dynamic-slice
  42.5 0.0 copy-done.2
  42.5 0.2 dynamic-update-slice.1
  42.8 0.0 copy-done.3
  42.8 0.2 dynamic-update-slice
  43.0 10.7 %all-reduce.2 = (s32[96]{0:T(128)S(1)}, s32[96]{0:T(128)S(1)}) all-reduce(s32[96]{0:T(128)S(1)} %dynamic-update-slice.1, s32[96]{0:T(128)S(1)} %dynamic-update-slice), channel_id=1, replica_groups=mesh['dp'=4,'vocab'=8] {'dp'}, use_global_device_ids=true, to_apply=%add.1 | all-reduce | flops 192 | bytes 1536
  53.7 0.1 broadcast_in_dim.6
  53.9 0.0 copy-done
  53.9 1.1 gather_fusion
  55.1 0.0 collective-permute-done
  55.1 10.3 %collective-permute-start.1 = (bf16[24,8192]{1,0:T(8,128)(2,1)S(1)}, bf16[24,8192]{1,0:T(8,128)(2,1)S(1)}, u32[]{:S(2)}, u32[]{:S(2)}) collective-permute-start(bf16[24,8192]{1,0:T(8,128)(2,1)S(1)} %collective-permute-done), channel_id=1, source_target_pairs={{0,8},{8,16},{16,24},{24,0},{1,9},{9,17},{17,25},{25,1},{2,10},{10... | collective-permute-start | bytes 1179656 | tf_op jit(solution)/shard_map/ppermute | solution.py:20
  65.4 9.6 %collective-permute-done.1 = bf16[24,8192]{1,0:T(8,128)(2,1)S(1)} collective-permute-done((bf16[24,8192]{1,0:T(8,128)(2,1)S(1)}, bf16[24,8192]{1,0:T(8,128)(2,1)S(1)}, u32[]{:S(2)}, u32[]{:S(2)}) %collective-permute-start.1) | collective-permute-done | bytes 393248 | tf_op jit(solution)/shard_map/ppermute | solution.py:20
  75.0 0.4 collective-permute-start.2
  75.5 19.8 %collective-permute-done.2 = bf16[24,8192]{1,0:T(8,128)(2,1)S(1)} collective-permute-done((bf16[24,8192]{1,0:T(8,128)(2,1)S(1)}, bf16[24,8192]{1,0:T(8,128)(2,1)S(1)}, u32[]{:S(2)}, u32[]{:S(2)}) %collective-permute-start.2) | collective-permute-done | bytes 393248 | tf_op jit(solution)/shard_map/ppermute | solution.py:20
  95.3 0.0 all-gather.5.cloned.1.call-done
  95.3 5.4 %fusion.13 = f32[96,512]{1,0:T(8,128)S(1)} fusion(bf16[96,8192]{1,0:T(8,128)(2,1)} %all-gather.5.cloned.1.call-done, bf16[8192,512]{1,0:T(8,128)(2,1)} %param.11), kind=kOutput, calls=%fused_computation.30 | convolution fusion | flops 805306368 | bytes 10158080 | tf_op jit(solution)/shard_map/dot_general | solution.py:53
  100.7 5.0 %fusion.12 = (f32[96]{0:T(128)S(1)}, f32[96,512]{1,0:T(8,128)S(1)}) fusion(f32[96,512]{1,0:T(8,128)S(1)} %fusion.13, bf16[96,8192]{1,0:T(8,128)(2,1)S(1)} %constant_dynamic-update-slice_fusion, bf16[8192,512]{1,0:T(8,128)(2,1)} %param.11), kind=kOutput, calls=%fused_computation.29 | convolution fusion | flops 805552000 | bytes 10355072 | tf_op jit(solution)/shard_map/dot_general | solution.py:54
  105.7 7.6 %all-gather.3.cloned.1.call-done = bf16[96,8192]{1,0:T(8,128)(2,1)} async-done(((bf16[24,8192]{1,0:T(8,128)(2,1)}), bf16[96,8192]{1,0:T(8,128)(2,1)}) %all-gather.3.cloned.1.call-update) | async-done | bytes 1572880 | tf_op jit(solution)/shard_map/all_gather | solution.py:46
  113.3 5.4 %fusion.11 = (f32[96]{0:T(128)S(1)}, f32[96,512]{1,0:T(8,128)S(1)}) fusion(bf16[96,8192]{1,0:T(8,128)(2,1)} %all-gather.3.cloned.1.call-done, bf16[8192,512]{1,0:T(8,128)(2,1)} %param.12), kind=kOutput, calls=%fused_computation.28 | convolution fusion | flops 805355392 | bytes 10158464 | tf_op jit(solution)/shard_map/dot_general | solution.py:56
  118.8 38.5 %all-reduce.4 = (f32[96]{0:T(128)S(1)}, f32[96]{0:T(128)S(1)}) all-reduce(f32[96]{0:T(128)S(1)} %get-tuple-element.25, f32[96]{0:T(128)S(1)} %get-tuple-element.27), channel_id=1, replica_groups=mesh['dp'=4,'vocab'=8] {'dp','vocab'}, use_global_device_ids=true, to_apply=%region_1.2 | all-reduce | flops 192 | bytes 1536 | tf_op jit(solution)/shard_map/pmax | solution.py:62
  157.3 0.3 fusion.9
  157.5 40.8 %all-reduce.3 = (f32[96]{0:T(128)S(1)}, f32[96]{0:T(128)S(1)}, f32[96]{0:T(128)S(1)}, f32[96]{0:T(128)S(1)}) all-reduce(f32[96]{0:T(128)S(1)} %get-tuple-element.12, f32[96]{0:T(128)S(1)} %get-tuple-element.13, f32[96]{0:T(128)S(1)} %get-tuple-element.14, f32[96]{0:T(128)S(1)} %get-tuple-element.11), channel_id=1, replica_groups=mesh['dp'=4,'vocab'=8] {'dp','vocab'}, use_global_device_ids=true, to_apply=%region_11.12 | all-reduce | flops 384 | bytes 3072 | tf_op jit(solution)/shard_map/psum | solution.py:67
  198.4 0.2 fusion.8
  198.6 7.8 %fusion.14 = f32[4,24,8,1024]{3,1,2,0:T(8,128)} fusion(bf16[4,24,512,1]{2,1,3,0:T(8,128)(2,1)S(1)} %bitcast.26, bf16[8,1024,512,1]{2,1,0,3:T(8,128)(2,1)} %bitcast.24), kind=kOutput, calls=%fused_computation.31 | convolution fusion | flops 805306368 | bytes 11632640 | tf_op jit(solution)/shard_map/atv,bdv->abtd/dot_general | solution.py:95
  206.4 0.0 copy-start.1
  206.4 0.0 reduce-scatter.2.cloned.1.call-update
  206.4 1.4 copy-done.1
  207.8 5.6 %fusion = bf16[8192,512]{0,1:T(8,128)(2,1)} fusion(bf16[96,512]{1,0:T(8,128)(2,1)S(1)} %fusion.8, bf16[96,8192]{1,0:T(8,128)(2,1)S(1)} %copy-done.1), kind=kOutput, calls=%fused_computation.2 | convolution fusion | flops 809500672 | bytes 10059776 | tf_op jit(solution)/shard_map/dot_general | solution.py:90
  213.4 12.0 %copy.12 = bf16[8192,512]{1,0:T(8,128)(2,1)} copy(bf16[8192,512]{0,1:T(8,128)(2,1)} %fusion) | data formatting | bytes 16777216
  225.4 0.6 dynamic_slice.3
  226.0 82.8 %reduce-scatter.2.cloned.1.call-done = f32[24,1024]{1,0:T(8,128)} async-done(((f32[768,1024]{1,0:T(8,128)}), f32[24,1024]{1,0:T(8,128)}) %reduce-scatter.2.cloned.1.call-update) | async-done | bytes 98320 | tf_op jit(solution)/shard_map/reduce_scatter | solution.py:99
  308.7 1.5 convert_element_type.20
  (10 shorter events, 0.2 us)
Async XLA Ops:
  7.2 46.8 %copy-start = (s32[16384]{0:T(1024)S(1)}, s32[16384]{0:T(1024)}, u32[]{:S(2)}) copy-start(s32[16384]{0:T(1024)} %param.14) | copy-start | bytes 196612
  7.2 34.1 %copy-start.4 = (u32[32]{0:T(128)S(1)}, u32[32]{0:T(128)}, u32[]{:S(2)}) copy-start(u32[32]{0:T(128)} %constant.74) | copy-start | bytes 388
  7.2 35.3 %copy-start.2 = (s32[24]{0:T(128)S(1)}, s32[24]{0:T(128)}, u32[]{:S(2)}) copy-start(s32[24]{0:T(128)} %param.13) | copy-start | bytes 292
  7.2 35.6 %copy-start.3 = (s32[24]{0:T(128)S(1)}, s32[24]{0:T(128)}, u32[]{:S(2)}) copy-start(s32[24]{0:T(128)} %param.15) | copy-start | bytes 292
  7.2 88.1 %all-gather.5.cloned.1.call-start = ((), (), s32[]{:S(2)}) async-start(), calls=%async_computation.2 | async-start | bytes 1966080 | tf_op jit(solution)/shard_map/all_gather | solution.py:44
  20.2 93.1 %all-gather.3.cloned.1.call-start = ((), (), s32[]{:S(2)}) async-start(), calls=%async_computation.1 | async-start | bytes 1966080 | tf_op jit(solution)/shard_map/all_gather | solution.py:46
  29.1 26.0 %collective-permute-start = (bf16[24,8192]{1,0:T(8,128)(2,1)S(1)}, bf16[24,8192]{1,0:T(8,128)(2,1)S(1)}, u32[]{:S(2)}, u32[]{:S(2)}) collective-permute-start(bf16[24,8192]{1,0:T(8,128)(2,1)S(1)} %all_gather.26), channel_id=1, source_target_pairs={{0,8},{8,16},{16,24},{24,0},{1,9},{9,17},{17,25},{25,1},{2,10},{10... | collective-permute-start | bytes 1179656 | tf_op jit(solution)/shard_map/ppermute | solution.py:20
  41.1 267.6 %reduce-scatter.2.cloned.1.call-start = ((), (), s32[]{:S(2)}) async-start(), calls=%async_computation.3 | async-start | bytes 3244032 | tf_op jit(solution)/shard_map/reduce_scatter | solution.py:99
  55.1 19.9 %collective-permute-start.1 = (bf16[24,8192]{1,0:T(8,128)(2,1)S(1)}, bf16[24,8192]{1,0:T(8,128)(2,1)S(1)}, u32[]{:S(2)}, u32[]{:S(2)}) collective-permute-start(bf16[24,8192]{1,0:T(8,128)(2,1)S(1)} %collective-permute-done), channel_id=1, source_target_pairs={{0,8},{8,16},{16,24},{24,0},{1,9},{9,17},{17,25},{25,1},{2,10},{10... | collective-permute-start | bytes 1179656 | tf_op jit(solution)/shard_map/ppermute | solution.py:20
  75.0 20.2 %collective-permute-start.2 = (bf16[24,8192]{1,0:T(8,128)(2,1)S(1)}, bf16[24,8192]{1,0:T(8,128)(2,1)S(1)}, u32[]{:S(2)}, u32[]{:S(2)}) collective-permute-start(bf16[24,8192]{1,0:T(8,128)(2,1)S(1)} %collective-permute-done.1), channel_id=1, source_target_pairs={{0,8},{8,16},{16,24},{24,0},{1,9},{9,17},{17,25},{25,1},{2,10},{10... | collective-permute-start | bytes 1179656 | tf_op jit(solution)/shard_map/ppermute | solution.py:20
  206.4 1.4 copy-start.1
Sparse Core Ops, SparseCore 0:
  20.3 46.6 all-gather.4
  68.5 44.7 all-gather.2
  206.5 102.1 reduce-scatter.1
